TPU v7x, 256 devices: a whole 4x4x8 slice. The times are simulated.
256 devices in a mesh: row: 64 (over y, z, core), col: 4 (over x).
Axes of the slice: x: 4, y: 4, z: 8, core: 2. Of those that a mesh axis runs over, the one named last changes fastest.
Arguments:
- leaf_grad: bfloat16 [256, 32, 1024], P('row', None, 'col'), may hold values from -6 to 6
- leaf_inv: bfloat16 [256, 1024, 1024], P('row', 'col'), as said below
- leaf_cpl: bfloat16 [256, 1024, 512], P('row', 'col'), may hold values from -0.046875 to 0.046875
- leaf_size: int32 [256], P('row'), may hold values from 256 to 1024, as said below
- leaf_parent: int32 [256], P('row'), may hold values from 0 to 3
- leaf_map: int32 [256, 512], P('row'), may hold values from 0 to 2047
- mid_grad: bfloat16 [32, 4, 2048], P(None, 'col', 'row'), may hold values from -6 to 6
- mid_inv: bfloat16 [4, 2048, 2048], P('col', 'row'), as said below
- mid_cpl: bfloat16 [4, 2048, 512], P('col', 'row'), may hold values from -0.125 to 0.125
- mid_map: int32 [4, 512], replicated, may hold values from 0 to 2047
- root_grad: bfloat16 [32, 2048], P(None, 'row'), may hold values from -6 to 6
- root_inv: bfloat16 [2048, 2048], P('row'), as said below
Outputs:
- leaf_x: float32 [256, 32, 1024], P('row', None, 'col')
- mid_x: float32 [32, 4, 2048], P(None, 'col', 'row')
- root_x: float32 [32, 2048], P(None, 'row')
Inputs may be any that keep to these rules, and one draw needn't show every extreme that they name: `leaf_size`: some leaf in every draw has 1024 live pivot columns. `leaf_map`: columns may repeat. `mid_map`: columns may repeat. `leaf_inv`: upper triangular; diagonal entries between 1 and 1.25, entries above the diagonal of scale 1024 ** -0.5. `mid_inv`: each front's block is upper triangular; diagonal entries between 1 and 1.25, entries above the diagonal of scale 2048 ** -0.5. `root_inv`: upper triangular; diagonal entries between 1 and 1.25, entries above the diagonal of scale 2048 ** -0.5.
All inputs are finite; a program needn't handle non-finite values.
Results may differ from a plain program's by a relative error of at most 0.012.
Values may be sent and summed in bfloat16 or wider, within the bound.
No kernel may reach another device: no remote copies, remote signals or barrier semaphores. Data moves between devices by JAX's collectives and lax.ppermute only.
A program may use at most 64 MiB of HBM per device.

v0:
```python
import jax
import jax.numpy as jnp
from jax import lax
from jax.sharding import PartitionSpec as P


def body(
    leaf_grad,
    leaf_inv,
    leaf_cpl,
    leaf_size,
    leaf_parent,
    leaf_map,
    mid_grad,
    mid_inv,
    mid_cpl,
    mid_map,
    root_grad,
    root_inv,
):
    ncolumns = lax.axis_size("col")
    row_id = lax.axis_index("row")
    col_id = lax.axis_index("col")
    nleaves = leaf_inv.shape[0]
    share_rows = leaf_inv.shape[1]
    nrhs = leaf_grad.shape[1]
    front = mid_inv.shape[2]
    mid_rows = mid_inv.shape[1]
    nmiddle = mid_map.shape[0]
    root_order = root_inv.shape[1]
    root_rows = root_inv.shape[0]
    inv_block = mid_inv[0]
    cpl_block = mid_cpl[0]
    first_cols = col_id * share_rows + lax.iota(jnp.int32, share_rows)
    live = (first_cols[None, :] < leaf_size[:, None])[:, None, :]
    partial_value = jnp.einsum(
        "lkp,lpq->lkq", leaf_grad, leaf_inv, preferred_element_type=jnp.float32
    )
    leaf_y = jnp.where(
        live, lax.psum_scatter(partial_value, "col", scatter_dimension=2, tiled=True), 0.0
    )
    leaf_yb = leaf_y.astype(jnp.bfloat16)
    shares = jnp.einsum("lkp,lpc->klc", leaf_yb, leaf_cpl, preferred_element_type=jnp.float32)
    placed_cols = (
        leaf_map // mid_rows * ncolumns + leaf_parent[:, None]
    ) * mid_rows + leaf_map % mid_rows
    targets = placed_cols.reshape(-1)
    spread = (
        jnp.zeros((nrhs, nmiddle * front), jnp.float32).at[:, targets].add(shares.reshape(nrhs, -1))
    )
    arrived = lax.psum_scatter(spread, ("row", "col"), scatter_dimension=1, tiled=True)
    mid_hb = (mid_grad[:, 0, :].astype(jnp.float32) - arrived).astype(jnp.bfloat16)
    mid_part = jnp.dot(mid_hb, inv_block, preferred_element_type=jnp.float32)
    mid_y = lax.psum_scatter(mid_part, "row", scatter_dimension=1, tiled=True)
    mid_yb = mid_y.astype(jnp.bfloat16)
    mid_share = jnp.dot(mid_yb, cpl_block, preferred_element_type=jnp.float32)
    root_cols = lax.dynamic_index_in_dim(mid_map, col_id, 0, keepdims=False)
    root_term = jnp.zeros((nrhs, root_order), jnp.float32).at[:, root_cols].add(mid_share)
    root_total = lax.psum(root_term, ("row", "col"))
    root_slice = lax.dynamic_slice_in_dim(root_total, row_id * root_rows, root_rows, 1)
    root_hb = (root_grad.astype(jnp.float32) - root_slice).astype(jnp.bfloat16)
    root_y = lax.psum(jnp.dot(root_hb, root_inv, preferred_element_type=jnp.float32), "row")
    root_yb = root_y.astype(jnp.bfloat16)
    root_x = jnp.einsum("kq,pq->kp", root_yb, root_inv, preferred_element_type=jnp.float32)
    root_all = lax.all_gather(root_x.astype(jnp.bfloat16), "row", axis=1, tiled=True)
    coupled = root_all[:, root_cols]
    mid_wb = (
        mid_y - jnp.einsum("kc,bc->kb", coupled, cpl_block, preferred_element_type=jnp.float32)
    ).astype(jnp.bfloat16)
    full_w = lax.all_gather(mid_wb, "row", axis=1, tiled=True)
    mid_x = jnp.einsum("kq,bq->kb", full_w, inv_block, preferred_element_type=jnp.float32)
    all_mid = lax.all_gather(mid_x.astype(jnp.bfloat16), ("row", "col"), axis=1, tiled=True)
    picked = all_mid[:, targets].reshape(nrhs, nleaves, -1)
    leaf_w = leaf_y - jnp.einsum(
        "klc,lpc->lkp", picked, leaf_cpl, preferred_element_type=jnp.float32
    )
    leaf_wb = jnp.where(live, leaf_w, 0.0).astype(jnp.bfloat16)
    leaf_x = jnp.einsum(
        "lkq,lpq->lkp",
        lax.all_gather(leaf_wb, "col", axis=2, tiled=True),
        leaf_inv,
        preferred_element_type=jnp.float32,
    )
    return (leaf_x, mid_x[:, None, :], root_x)


def solution(mesh):
    placed = (
        P("row", None, "col"),
        P("row", "col", None),
        P("row", "col", None),
        P("row"),
        P("row"),
        P("row", None),
        P(None, "col", "row"),
        P("col", "row", None),
        P("col", "row", None),
        P(),
        P(None, "row"),
        P("row", None),
    )
    return jax.shard_map(
        body,
        mesh=mesh,
        in_specs=placed,
        out_specs=(P("row", None, "col"), P(None, "col", "row"), P(None, "row")),
        check_vma=False,
    )
```

profile of v0, /device:TPU:8, one launch (start us, length us, event | category | flops | bytes accessed | tf_op | source)
XLA Modules:
  0.0 2242.4 jit_solution(18431036264109343897)
XLA Ops:
  7.2 0.0 copy-start
  7.2 0.0 copy-start.11
  7.2 0.0 copy-start.14
  7.2 0.0 copy-start.15
  7.2 0.0 copy-start.1
  7.2 0.0 reduce-scatter.6.cloned.1.call-start
  7.3 1.5 copy-done
  8.8 2.1 fusion.32
  10.9 0.0 reduce-scatter.6.cloned.1.call-update
  10.9 0.0 reduce-scatter.8.cloned.1.call-start
  10.9 0.0 copy-done.11
  11.0 0.0 copy-done.14
  11.0 0.1 fusion.21
  11.1 0.0 copy-done.15
  11.1 0.1 broadcast_compare_fusion
  11.2 0.0 copy-start.7
  11.2 26.7 %reduce-scatter.6.cloned.1.call-done = f32[4,32,256]{2,1,0:T(8,128)} async-done(((f32[4,32,1024]{2,1,0:T(8,128)}), f32[4,32,256]{2,1,0:T(8,128)}) %reduce-scatter.6.cloned.1.call-update) | async-done | bytes 131088 | tf_op jit(solution)/shard_map/reduce_scatter | solution.py:40
  37.9 0.0 copy-done.9
  37.9 0.0 copy-done.1
  37.9 1.2 convolution_bitcast_fusion.1
  39.1 1.3 copy.29
  40.4 14.0 scatter_custom_fusion
  54.4 0.0 copy-done.7
  54.4 0.0 reduce-scatter.8.cloned.1.call-update
  54.4 0.0 copy-start.5
  54.4 0.0 reduce-scatter.10.cloned.1.call-start
  54.5 0.6 copy-done.12
  55.1 0.1 copy.27
  55.2 1119.9 %reduce-scatter.8.cloned.1.call-done = f32[32,32]{0,1:T(8,128)} async-done(((f32[32,8192]{0,1:T(8,128)}), f32[32,32]{0,1:T(8,128)}) %reduce-scatter.8.cloned.1.call-update) | async-done | bytes 4112 | tf_op jit(solution)/shard_map/reduce_scatter | solution.py:51
  1175.1 0.0 copy-done.4
  1175.1 2.0 convolution_bitcast_fusion
  1177.2 0.0 reduce-scatter.10.cloned.1.call-update
  1177.2 0.0 all-reduce.3.cloned.1.call-start
  1177.2 0.7 compare_select_fusion.1
  1178.0 286.1 %reduce-scatter.10.cloned.1.call-done = f32[32,32]{1,0:T(8,128)} async-done(((f32[2048,32]{1,0:T(8,128)}), f32[32,32]{1,0:T(8,128)}) %reduce-scatter.10.cloned.1.call-update) | async-done | bytes 4112
  1464.0 0.8 copy.39
  1464.8 0.0 copy-done.5
  1464.8 0.1 convolution_bitcast_fusion.2
  1464.9 0.9 copy.31
  1465.8 3.6 scatter_custom_fusion.1
  1469.4 0.0 all-reduce.3.cloned.1.call-update
  1469.4 0.0 copy-done.8
  1469.4 0.6 broadcast_clamp_fusion
  1470.0 0.0 copy-done.13
  1470.0 0.7 copy.30
  1470.7 0.6 pad_clamp_fusion
  1471.3 254.1 %all-reduce.3.cloned.1.call-done = f32[32,2048]{0,1:T(8,128)} async-done(((f32[32,2048]{0,1:T(8,128)}), f32[32,2048]{0,1:T(8,128)}) %all-reduce.3.cloned.1.call-update) | async-done | bytes 262160 | tf_op jit(solution)/shard_map/psum | solution.py:59
  1725.4 0.9 fusion.22
  1726.3 214.4 %all-reduce.4 = bf16[32,2048]{1,0:T(8,128)(2,1)S(1)} all-reduce(f32[32,2048]{1,0:T(8,128)S(1)} %fusion.22), channel_id=1, replica_groups=mesh['row'=64,'col'=4] {'row'}, use_global_device_ids=true, to_apply=%region_6.7 | all-reduce | flops 65536 | bytes 393216 | tf_op jit(solution)/shard_map/psum | solution.py:62
  1940.7 1.7 fusion.30
  1942.4 0.1 copy.32
  1942.5 87.3 %all_gather.12 = bf16[32,2048]{0,1:T(8,128)(2,1)} all-gather(bf16[32,32]{0,1:T(8,128)(2,1)S(1)} %copy.32), channel_id=1, replica_groups=mesh['row'=64,'col'=4] {'row'}, dimensions={1}, use_global_device_ids=true | all-gather | bytes 133120 | tf_op jit(solution)/shard_map/all_gather | solution.py:65
  2029.8 2.3 gather_fusion
  2032.1 0.9 fusion.4
  2033.0 0.1 copy.33
  2033.1 47.8 %all_gather.13 = bf16[32,2048]{0,1:T(8,128)(2,1)S(1)} all-gather(bf16[32,32]{0,1:T(8,128)(2,1)S(1)} %copy.33), channel_id=1, replica_groups=mesh['row'=64,'col'=4] {'row'}, dimensions={1}, use_global_device_ids=true | all-gather | bytes 133120 | tf_op jit(solution)/shard_map/all_gather | solution.py:70
  2080.9 1.8 fusion.31
  2082.7 0.1 copy.34
  2082.8 128.3 %all_gather.14 = bf16[32,8192]{0,1:T(8,128)(2,1)} all-gather(bf16[32,32]{0,1:T(8,128)(2,1)S(1)} %copy.34), channel_id=1, replica_groups=mesh['row'=64,'col'=4] {'row','col'}, dimensions={1}, use_global_device_ids=true | all-gather | bytes 526336 | tf_op jit(solution)/shard_map/all_gather | solution.py:72
  2211.1 9.5 gather_fusion.1
  2220.6 0.0 copy-done.2
  2220.6 1.5 fusion.3
  2222.1 12.4 all_gather.15
  2234.4 1.4 fusion.33
  (16 shorter events, 0.1 us)
Async XLA Ops:
  7.2 1.6 copy-start
  7.2 3.8 copy-start.11
  7.2 3.8 copy-start.14
  7.2 3.9 copy-start.15
  7.2 30.7 %copy-start.1 = (bf16[4,256,512]{2,1,0:T(8,128)(2,1)S(1)}, bf16[4,256,512]{2,1,0:T(8,128)(2,1)}, u32[]{:S(2)}) copy-start(bf16[4,256,512]{2,1,0:T(8,128)(2,1)} %param.14) | copy-start | bytes 3145732
  7.2 30.7 %reduce-scatter.6.cloned.1.call-start = ((), (), s32[]{:S(2)}) async-start(), calls=%async_computation.3 | async-start | bytes 655360 | tf_op jit(solution)/shard_map/reduce_scatter | solution.py:40
  10.9 1164.2 %reduce-scatter.8.cloned.1.call-start = ((), (), s32[]{:S(2)}) async-start(), calls=%async_computation.4 | async-start | bytes 4210688 | tf_op jit(solution)/shard_map/reduce_scatter | solution.py:51
  11.2 26.7 %copy-start.9 = (pred[4,256]{1,0:T(4,128)(4,1)}, pred[4,256]{1,0:T(4,128)(4,1)S(1)}, u32[]{:S(2)}) copy-start(pred[4,256]{1,0:T(4,128)(4,1)S(1)} %broadcast_compare_fusion) | copy-start | bytes 3076
  11.2 43.2 %copy-start.7 = (s32[2048,1]{0,1:T(1,128)}, s32[2048,1]{0,1:T(1,128)S(1)}, u32[]{:S(2)}) copy-start(s32[2048,1]{0,1:T(1,128)S(1)} %compare_select_fusion) | copy-start | bytes 24580
  54.4 0.7 copy-start.12
  54.4 1120.7 %copy-start.4 = (bf16[1,32,2048]{2,1,0:T(8,128)(2,1)S(1)}, bf16[1,32,2048]{2,1,0:T(8,128)(2,1)}, u32[]{:S(2)}) copy-start(bf16[1,32,2048]{2,1,0:T(8,128)(2,1)} %param.19) | copy-start | bytes 393220
  54.4 1410.4 %copy-start.5 = (bf16[1,32,512]{2,1,0:T(8,128)(2,1)S(1)}, bf16[1,32,512]{2,1,0:T(8,128)(2,1)}, u32[]{:S(2)}) copy-start(bf16[1,32,512]{2,1,0:T(8,128)(2,1)} %param.20) | copy-start | bytes 98308
  54.4 1409.6 %reduce-scatter.10.cloned.1.call-start = ((), (), s32[]{:S(2)}) async-start(), calls=%async_computation.6 | async-start | bytes 1064960
  1177.2 292.3 %copy-start.8 = (s32[2048,1]{0,1:T(1,128)S(1)}, s32[2048,1]{0,1:T(1,128)}, u32[]{:S(2)}) copy-start(s32[2048,1]{0,1:T(1,128)} %copy-done.7) | copy-start | bytes 24580
  1177.2 292.9 %copy-start.13 = (bf16[32,32]{1,0:T(8,128)(2,1)S(1)}, bf16[32,32]{1,0:T(8,128)(2,1)}, u32[]{:S(2)}) copy-start(bf16[32,32]{1,0:T(8,128)(2,1)} %param.22) | copy-start | bytes 6148
  1177.2 548.2 %copy-start.3 = (bf16[32,2048]{1,0:T(8,128)(2,1)S(1)}, bf16[32,2048]{1,0:T(8,128)(2,1)}, u32[]{:S(2)}) copy-start(bf16[32,2048]{1,0:T(8,128)(2,1)} %param.23) | copy-start | bytes 393220
  1177.2 548.2 %all-reduce.3.cloned.1.call-start = ((), (), s32[]{:S(2)}) async-start(), calls=%async_computation.5 | async-start | bytes 2097152 | tf_op jit(solution)/shard_map/psum | solution.py:59
  1942.5 268.6 %copy-start.6 = (s32[2048]{0:T(1024)S(1)}, s32[2048]{0:T(1024)}, u32[]{:S(2)}) copy-start(s32[2048]{0:T(1024)} %broadcast_clamp_fusion) | copy-start | bytes 24580
  2080.9 139.7 %copy-start.2 = (f32[4,32,256]{2,1,0:T(8,128)S(1)}, f32[4,32,256]{2,1,0:T(8,128)}, u32[]{:S(2)}) copy-start(f32[4,32,256]{2,1,0:T(8,128)} %reduce-scatter.6.cloned.1.call-done) | copy-start | bytes 393220
  2080.9 139.7 %copy-start.10 = (pred[4,256]{1,0:T(4,128)(4,1)S(1)}, pred[4,256]{1,0:T(4,128)(4,1)}, u32[]{:S(2)}) copy-start(pred[4,256]{1,0:T(4,128)(4,1)} %copy-done.9) | copy-start | bytes 3076
Sparse Core Ops, SparseCore 0:
  11.0 26.8 reduce-scatter.5
  54.5 1120.5 reduce-scatter.7
  1179.6 284.3 reduce-scatter.9
  1470.2 255.1 all-reduce.2
where the time goes:
time: 2240 us
  waiting for transfers between devices  1690 us (75%)
  blocking collectives  490 us (22%)
    reduce_scatter x1, waiting for transfers between devices, body(): lax.psum_scatter(spread, ('row', 'col'), scatter_dimension=1, tiled=True)  1120 us
    unnamed x5, waiting for transfers between devices  286 us
    psum x1, waiting for transfers between devices, body(): root_total = lax.psum(root_term, ('row', 'col'))  254 us
    psum x1, blocking collectives, body(): lax.psum(jnp.dot(root_hb, root_inv, preferred_element_type=jnp.float32),...  214 us
    all_gather x1, blocking collectives, body(): lax.all_gather(mid_x.astype(jnp.bfloat16), ('row', 'col'), axis=1, tiled=...  128 us
    all_gather x1, blocking collectives, body(): lax.all_gather(root_x.astype(jnp.bfloat16), 'row', axis=1, tiled=True)  87.3 us
    all_gather x1, blocking collectives, body(): full_w = lax.all_gather(mid_wb, 'row', axis=1, tiled=True)  47.8 us
  transfers between devices with their start and end apart: 4, of which 4 were waited for; matrix products, arithmetic and copies ran while one was open for 0% of the time, Pallas kernels for 0%

commit v1 on v0

--- a/solution.py
+++ b/solution.py
@@ -56,7 +56,7 @@
     mid_share = jnp.dot(mid_yb, cpl_block, preferred_element_type=jnp.float32)
     root_cols = lax.dynamic_index_in_dim(mid_map, col_id, 0, keepdims=False)
     root_term = jnp.zeros((nrhs, root_order), jnp.float32).at[:, root_cols].add(mid_share)
-    root_total = lax.psum(root_term, ("row", "col"))
+    root_total = lax.psum(lax.psum(root_term, "col"), "row")
     root_slice = lax.dynamic_slice_in_dim(root_total, row_id * root_rows, root_rows, 1)
     root_hb = (root_grad.astype(jnp.float32) - root_slice).astype(jnp.bfloat16)
     root_y = lax.psum(jnp.dot(root_hb, root_inv, preferred_element_type=jnp.float32), "row")

time: 2240 us -> 2220 us (level)
    psum x1 -> x2, waiting for transfers between devices: 254 us -> 238 us  [body(): root_total = lax.psum(lax.psum(root_term, 'col'), 'row')]
    unnamed x5 -> x6, waiting for transfers between devices: 286 us -> 286 us
  transfers between devices with their start and end apart: 4 -> 5, of which waited for: 4 -> 5; matrix products, arithmetic and copies ran while one was open for 0% -> 0% of each run, Pallas kernels for 0% -> 0%
where the time goes in v1:
time: 2220 us
  waiting for transfers between devices  1670 us (75%)
  blocking collectives  488 us (22%)
    reduce_scatter x1, waiting for transfers between devices, body(): lax.psum_scatter(spread, ('row', 'col'), scatter_dimension=1, tiled=True)  1120 us
    unnamed x6, waiting for transfers between devices  286 us
    psum x2, waiting for transfers between devices, body(): root_total = lax.psum(lax.psum(root_term, 'col'), 'row')  238 us
    psum x1, blocking collectives, body(): lax.psum(jnp.dot(root_hb, root_inv, preferred_element_type=jnp.float32),...  212 us
    all_gather x1, blocking collectives, body(): lax.all_gather(mid_x.astype(jnp.bfloat16), ('row', 'col'), axis=1, tiled=...  128 us
    all_gather x1, blocking collectives, body(): lax.all_gather(root_x.astype(jnp.bfloat16), 'row', axis=1, tiled=True)  87.3 us
    all_gather x1, blocking collectives, body(): full_w = lax.all_gather(mid_wb, 'row', axis=1, tiled=True)  47.8 us
  transfers between devices with their start and end apart: 5, of which 5 were waited for; matrix products, arithmetic and copies ran while one was open for 0% of the time, Pallas kernels for 0%

profile of v1, /device:TPU:8, one launch (start us, length us, event | category | flops | bytes accessed | tf_op | source)
XLA Modules:
  0.0 2224.1 jit_solution(10069243452047572523)
XLA Ops:
  7.2 0.0 copy-start
  7.2 0.0 copy-start.11
  7.2 0.0 copy-start.14
  7.2 0.0 copy-start.15
  7.2 0.0 copy-start.1
  7.2 0.0 reduce-scatter.6.cloned.1.call-start
  7.3 1.5 copy-done
  8.8 2.1 fusion.32
  10.9 0.0 reduce-scatter.6.cloned.1.call-update
  10.9 0.0 reduce-scatter.8.cloned.1.call-start
  10.9 0.0 copy-done.11
  11.0 0.0 copy-done.14
  11.0 0.1 fusion.21
  11.1 0.1 broadcast_compare_fusion
  11.2 0.0 copy-start.7
  11.2 26.7 %reduce-scatter.6.cloned.1.call-done = f32[4,32,256]{2,1,0:T(8,128)} async-done(((f32[4,32,1024]{2,1,0:T(8,128)}), f32[4,32,256]{2,1,0:T(8,128)}) %reduce-scatter.6.cloned.1.call-update) | async-done | bytes 131088 | tf_op jit(solution)/shard_map/reduce_scatter | solution.py:40
  37.9 0.0 copy-done.1
  37.9 1.2 convolution_bitcast_fusion.1
  39.1 1.3 copy.29
  40.4 14.0 scatter_custom_fusion
  54.4 0.0 reduce-scatter.8.cloned.1.call-update
  54.4 0.0 copy-start.5
  54.4 0.0 reduce-scatter.10.cloned.1.call-start
  54.5 0.6 copy-done.12
  55.1 0.1 copy.27
  55.2 1119.9 %reduce-scatter.8.cloned.1.call-done = f32[32,32]{0,1:T(8,128)} async-done(((f32[32,8192]{0,1:T(8,128)}), f32[32,32]{0,1:T(8,128)}) %reduce-scatter.8.cloned.1.call-update) | async-done | bytes 4112 | tf_op jit(solution)/shard_map/reduce_scatter | solution.py:51
  1175.1 2.0 convolution_bitcast_fusion
  1177.2 0.0 reduce-scatter.10.cloned.1.call-update
  1177.2 0.0 copy-start.13
  1177.2 0.0 copy-start.3
  1177.2 0.0 all-reduce.4.cloned.1.call-start
  1177.3 0.7 compare_select_fusion.1
  1178.0 286.1 %reduce-scatter.10.cloned.1.call-done = f32[32,32]{1,0:T(8,128)} async-done(((f32[2048,32]{1,0:T(8,128)}), f32[32,32]{1,0:T(8,128)}) %reduce-scatter.10.cloned.1.call-update) | async-done | bytes 4112
  1464.0 0.8 copy.39
  1464.8 0.1 convolution_bitcast_fusion.2
  1464.9 0.8 copy.31
  1465.8 3.7 scatter_custom_fusion.1
  1469.5 0.0 all-reduce.4.cloned.1.call-update
  1469.5 0.0 all-reduce.6.cloned.1.call-start
  1469.5 50.1 %all-reduce.4.cloned.1.call-done = f32[32,2048]{0,1:T(8,128)} async-done(((f32[32,2048]{0,1:T(8,128)}), f32[32,2048]{0,1:T(8,128)}) %all-reduce.4.cloned.1.call-update) | async-done | bytes 262160 | tf_op jit(solution)/shard_map/psum | solution.py:59
  1519.7 0.0 all-reduce.6.cloned.1.call-update
  1519.7 0.0 copy-done.8
  1519.7 0.6 broadcast_clamp_fusion
  1520.3 0.7 copy.30
  1521.0 0.6 pad_clamp_fusion
  1521.6 187.4 %all-reduce.6.cloned.1.call-done = f32[32,2048]{0,1:T(8,128)} async-done(((f32[32,2048]{0,1:T(8,128)}), f32[32,2048]{0,1:T(8,128)}) %all-reduce.6.cloned.1.call-update) | async-done | bytes 262160 | tf_op jit(solution)/shard_map/psum | solution.py:59
  1709.0 0.9 fusion.22
  1710.0 212.3 %all-reduce.7 = bf16[32,2048]{1,0:T(8,128)(2,1)S(1)} all-reduce(f32[32,2048]{1,0:T(8,128)S(1)} %fusion.22), channel_id=1, replica_groups=mesh['row'=64,'col'=4] {'row'}, use_global_device_ids=true, to_apply=%region_7.8 | all-reduce | flops 65536 | bytes 393216 | tf_op jit(solution)/shard_map/psum | solution.py:62
  1922.3 1.7 fusion.30
  1923.9 0.1 copy.32
  1924.0 87.3 %all_gather.12 = bf16[32,2048]{0,1:T(8,128)(2,1)} all-gather(bf16[32,32]{0,1:T(8,128)(2,1)S(1)} %copy.32), channel_id=1, replica_groups=mesh['row'=64,'col'=4] {'row'}, dimensions={1}, use_global_device_ids=true | all-gather | bytes 133120 | tf_op jit(solution)/shard_map/all_gather | solution.py:65
  2011.3 2.3 gather_fusion
  2013.6 0.9 fusion.4
  2014.6 0.1 copy.33
  2014.6 47.8 %all_gather.13 = bf16[32,2048]{0,1:T(8,128)(2,1)S(1)} all-gather(bf16[32,32]{0,1:T(8,128)(2,1)S(1)} %copy.33), channel_id=1, replica_groups=mesh['row'=64,'col'=4] {'row'}, dimensions={1}, use_global_device_ids=true | all-gather | bytes 133120 | tf_op jit(solution)/shard_map/all_gather | solution.py:70
  2062.4 1.8 fusion.31
  2064.3 0.1 copy.34
  2064.4 128.4 %all_gather.14 = bf16[32,8192]{0,1:T(8,128)(2,1)} all-gather(bf16[32,32]{0,1:T(8,128)(2,1)S(1)} %copy.34), channel_id=1, replica_groups=mesh['row'=64,'col'=4] {'row','col'}, dimensions={1}, use_global_device_ids=true | all-gather | bytes 526336 | tf_op jit(solution)/shard_map/all_gather | solution.py:72
  2192.8 0.0 copy-done.6
  2192.8 9.5 gather_fusion.1
  2202.3 0.0 copy-done.10
  2202.3 1.5 fusion.3
  2203.8 12.4 all_gather.15
  2216.2 1.4 fusion.33
  (19 shorter events, 0.1 us)
Async XLA Ops:
  7.2 1.6 copy-start
  7.2 3.8 copy-start.11
  7.2 3.8 copy-start.14
  7.2 3.9 copy-start.15
  7.2 30.7 %copy-start.1 = (bf16[4,256,512]{2,1,0:T(8,128)(2,1)S(1)}, bf16[4,256,512]{2,1,0:T(8,128)(2,1)}, u32[]{:S(2)}) copy-start(bf16[4,256,512]{2,1,0:T(8,128)(2,1)} %param.14) | copy-start | bytes 3145732
  7.2 30.7 %reduce-scatter.6.cloned.1.call-start = ((), (), s32[]{:S(2)}) async-start(), calls=%async_computation.3 | async-start | bytes 655360 | tf_op jit(solution)/shard_map/reduce_scatter | solution.py:40
  10.9 1164.2 %reduce-scatter.8.cloned.1.call-start = ((), (), s32[]{:S(2)}) async-start(), calls=%async_computation.4 | async-start | bytes 4210688 | tf_op jit(solution)/shard_map/reduce_scatter | solution.py:51
  11.2 26.7 %copy-start.9 = (pred[4,256]{1,0:T(4,128)(4,1)}, pred[4,256]{1,0:T(4,128)(4,1)S(1)}, u32[]{:S(2)}) copy-start(pred[4,256]{1,0:T(4,128)(4,1)S(1)} %broadcast_compare_fusion) | copy-start | bytes 3076
  11.2 43.2 %copy-start.7 = (s32[2048,1]{0,1:T(1,128)}, s32[2048,1]{0,1:T(1,128)S(1)}, u32[]{:S(2)}) copy-start(s32[2048,1]{0,1:T(1,128)S(1)} %compare_select_fusion) | copy-start | bytes 24580
  54.4 0.7 copy-start.12
  54.4 1120.7 %copy-start.4 = (bf16[1,32,2048]{2,1,0:T(8,128)(2,1)S(1)}, bf16[1,32,2048]{2,1,0:T(8,128)(2,1)}, u32[]{:S(2)}) copy-start(bf16[1,32,2048]{2,1,0:T(8,128)(2,1)} %param.19) | copy-start | bytes 393220
  54.4 1410.4 %copy-start.5 = (bf16[1,32,512]{2,1,0:T(8,128)(2,1)S(1)}, bf16[1,32,512]{2,1,0:T(8,128)(2,1)}, u32[]{:S(2)}) copy-start(bf16[1,32,512]{2,1,0:T(8,128)(2,1)} %param.20) | copy-start | bytes 98308
  54.4 1409.6 %reduce-scatter.10.cloned.1.call-start = ((), (), s32[]{:S(2)}) async-start(), calls=%async_computation.7 | async-start | bytes 1064960
  1177.2 342.5 %copy-start.8 = (s32[2048,1]{0,1:T(1,128)S(1)}, s32[2048,1]{0,1:T(1,128)}, u32[]{:S(2)}) copy-start(s32[2048,1]{0,1:T(1,128)} %copy-done.7) | copy-start | bytes 24580
  1177.2 343.1 %copy-start.13 = (bf16[32,32]{1,0:T(8,128)(2,1)S(1)}, bf16[32,32]{1,0:T(8,128)(2,1)}, u32[]{:S(2)}) copy-start(bf16[32,32]{1,0:T(8,128)(2,1)} %param.22) | copy-start | bytes 6148
  1177.2 531.8 %copy-start.3 = (bf16[32,2048]{1,0:T(8,128)(2,1)S(1)}, bf16[32,2048]{1,0:T(8,128)(2,1)}, u32[]{:S(2)}) copy-start(bf16[32,2048]{1,0:T(8,128)(2,1)} %param.23) | copy-start | bytes 393220
  1177.2 342.5 %all-reduce.4.cloned.1.call-start = ((), (), s32[]{:S(2)}) async-start(), calls=%async_computation.5 | async-start | bytes 2097152 | tf_op jit(solution)/shard_map/psum | solution.py:59
  1469.5 239.5 %all-reduce.6.cloned.1.call-start = ((), (), s32[]{:S(2)}) async-start(), calls=%async_computation.6 | async-start | bytes 2097152 | tf_op jit(solution)/shard_map/psum | solution.py:59
  1924.0 268.8 %copy-start.6 = (s32[2048]{0:T(1024)S(1)}, s32[2048]{0:T(1024)}, u32[]{:S(2)}) copy-start(s32[2048]{0:T(1024)} %broadcast_clamp_fusion) | copy-start | bytes 24580
  2062.4 139.9 %copy-start.2 = (f32[4,32,256]{2,1,0:T(8,128)S(1)}, f32[4,32,256]{2,1,0:T(8,128)}, u32[]{:S(2)}) copy-start(f32[4,32,256]{2,1,0:T(8,128)} %reduce-scatter.6.cloned.1.call-done) | copy-start | bytes 393220
  2062.4 139.9 %copy-start.10 = (pred[4,256]{1,0:T(4,128)(4,1)S(1)}, pred[4,256]{1,0:T(4,128)(4,1)}, u32[]{:S(2)}) copy-start(pred[4,256]{1,0:T(4,128)(4,1)} %copy-done.9) | copy-start | bytes 3076
Sparse Core Ops, SparseCore 0:
  11.0 26.8 reduce-scatter.5
  54.5 1120.5 reduce-scatter.7
  1179.6 284.3 reduce-scatter.9
  1469.6 50.0 all-reduce.3
  1522.9 186.0 all-reduce.5
